TPU v7x, 512 devices: a whole 4x8x8 slice. The times are simulated.
512 devices in a mesh: rep: 16 (over y, core), tp: 32 (over z, x).
Axes of the slice: x: 4, y: 8, z: 8, core: 2. Of those that a mesh axis runs over, the one named last changes fastest.
Arguments:
- tokens: bfloat16 [8192, 8192], P('rep', 'tp'), may hold values from -6 to 6
- base_weight: bfloat16 [8192, 8192], P(None, 'tp'), may hold values from -0.0625 to 0.0625
- delta: bfloat16 [48, 64, 2, 128, 128], P('rep', 'tp'), may hold values from -0.375 to 0.375
- live_blocks: int32 [48, 64, 2], P(None, 'tp'), may hold values from 0 to 63, as said below
- row_variant: int32 [8192, 1], P('rep'), may hold values from 0 to 47; in each aligned block of 512 rows (0 to 511, 512 to 1023, ...) at most 21 rows name the same one
Outputs:
- projected: bfloat16 [8192, 8192], P('rep', 'tp')
Inputs may be any that keep to these rules, and one draw needn't show every extreme that they name: `live_blocks`: the 2 block rows listed for one variant and column block are distinct. `row_variant`: among the rows of one index of rep no variant appears more than 21 times, and some variant appears exactly 21 times.
All inputs are finite; a program needn't handle non-finite values.
Results may differ from a plain program's by a relative error of at most 0.0039.
Values may be sent and summed in bfloat16 or wider, within the bound.
A program may use at most 128 MiB of HBM per device.

v0:
```python
import jax
import jax.numpy as jnp
from jax import lax
from jax.sharding import PartitionSpec as P


def multiply(received, weight_tables):
    sources, local_variants, slot_count, feat_width = received.shape
    col_blocks = weight_tables.shape[1]
    block_size = weight_tables.shape[3]
    shaped = received.reshape(
        sources, local_variants, slot_count, col_blocks, feat_width // col_blocks
    )
    flat_weights = weight_tables.reshape(
        local_variants, col_blocks, feat_width // col_blocks, block_size
    )
    result = jnp.einsum(
        "auncf,ucfb->auncb", shaped, flat_weights, preferred_element_type=jnp.float32
    )
    return result.astype(jnp.bfloat16).reshape(
        sources, local_variants, slot_count, col_blocks * block_size
    )


def local(tokens, base_weight, delta, live_blocks, row_variant):
    rep_count = lax.axis_size("rep")
    local_variants = delta.shape[0]
    col_blocks = delta.shape[1]
    live_count = delta.shape[2]
    block_size = delta.shape[3]
    variants = local_variants * rep_count
    row_count = tokens.shape[0]
    capacity = max(2, 2 * row_count // variants)
    feat_width = col_blocks * live_count * block_size
    features_all = lax.all_gather(tokens, "tp", axis=1, tiled=True)
    base_part = jnp.dot(features_all, base_weight, preferred_element_type=jnp.float32)
    variant = row_variant[:, 0]
    onehot = (variant[:, None] == jnp.arange(variants, dtype=jnp.int32)[None, :]).astype(jnp.int32)
    row_rank = jnp.sum((jnp.cumsum(onehot, axis=0) - 1) * onehot, axis=1)
    slot_index = variant * capacity + row_rank
    tile_indices = jnp.take(live_blocks, variant, axis=0).reshape(
        row_count, col_blocks * live_count
    )
    blocks_view = features_all.reshape(row_count, features_all.shape[1] // block_size, block_size)
    picked = jnp.take_along_axis(blocks_view, tile_indices[:, :, None], axis=1).reshape(
        row_count, feat_width
    )
    outgoing = jnp.zeros((variants * capacity, feat_width), jnp.bfloat16).at[slot_index].set(picked)
    all_deltas = lax.all_gather(delta, "rep", axis=0, tiled=True)
    returned = multiply(outgoing.reshape(1, variants, capacity, feat_width), all_deltas)
    returned_flat = returned.reshape(variants * capacity, col_blocks * block_size)
    correction_summand = jnp.take(returned_flat, slot_index, axis=0)
    return (base_part + correction_summand.astype(jnp.float32)).astype(jnp.bfloat16)


def solution(mesh):
    placed = (
        P("rep", "tp"),
        P(None, "tp"),
        P("rep", "tp", None, None, None),
        P(None, "tp", None),
        P("rep", None),
    )
    return jax.shard_map(
        local, mesh=mesh, in_specs=placed, out_specs=P("rep", "tp"), check_vma=False
    )
```

profile of v0, /device:TPU:1, one launch (start us, length us, event | category | flops | bytes accessed | tf_op | source)
XLA Modules:
  0.0 194.5 jit_solution(5336732794186079991)
XLA Ops:
  6.5 0.7 all-gather.3.cloned.1.call-update
  7.3 0.7 all-gather.5.cloned.1.call-update
  8.0 0.7 fusion.9
  8.7 1.2 reduce-window.6
  9.9 0.2 slice_reduce_fusion
  10.2 0.8 copy.20
  11.0 0.8 fusion.8
  11.7 0.7 and_reduce_fusion
  12.5 2.1 %gather_fusion = s32[512,2,2]{2,1,0:T(2,128)S(1)} fusion(s32[48,2,2]{2,1,0:T(2,128)S(1)} %copy.20, s32[1024]{0:T(1024)S(1)} %pad_clamp_fusion.1), kind=kCustom, calls=%fused_computation | custom fusion | bytes 18432 | tf_op jit(solution)/shard_map/jit(_take)/gather | solution.py:41
  14.6 0.2 copy.21
  14.8 0.1 copy.24
  15.0 0.2 reshape.171
  15.2 0.2 copy.22
  15.4 105.8 %all-gather.3.cloned.1.call-done = bf16[512,8192]{1,0:T(8,128)(2,1)} async-done(((bf16[512,256]{1,0:T(8,128)(2,1)}), bf16[512,8192]{1,0:T(8,128)(2,1)}) %all-gather.3.cloned.1.call-update) | async-done | bytes 8388624 | tf_op jit(solution)/shard_map/all_gather | solution.py:35
  121.1 9.3 %copy.28 = bf16[64,8,64,128]{3,2,1,0:T(8,128)(2,1)} copy(bf16[64,8,64,128]{3,1,2,0:T(8,128)(2,1)} %bitcast.50) | data formatting | bytes 16777216
  130.4 24.3 %gather_fusion.2 = bf16[2048,128]{1,0:T(8,128)(2,1)S(1)} fusion(bf16[512,64,128]{2,1,0:T(8,128)(2,1)} %bitcast.48, s32[2048]{0:T(1024)S(1)} %reshape.171), kind=kCustom, calls=%fused_computation.2 | custom fusion | bytes 1064960 | tf_op jit(solution)/shard_map/jit(take_along_axis)/gather | solution.py:45
  154.8 1.6 broadcast_select_fusion
  156.4 2.7 %scatter_custom_fusion = bf16[1008,512]{1,0:T(8,128)(2,1)S(1)} fusion(s32[512]{0:T(512)S(1)} %bitcast.58, bf16[64,8,4,128]{3,2,1,0:T(4,128)(2,1)S(1)} %bitcast.52, bf16[]{:T(256)} %constant.50.clone.1), kind=kCustom, calls=%fused_computation.9 | custom fusion | bytes 1556482 | tf_op jit(solution)/shard_map/scatter | solution.py:48
  159.1 0.2 reshape.153
  159.4 14.4 %all-gather.5.cloned.1.call-done = bf16[48,2,2,128,128]{4,3,2,1,0:T(8,128)(2,1)} async-done(((bf16[3,2,2,128,128]{4,3,2,1,0:T(8,128)(2,1)}), bf16[48,2,2,128,128]{4,3,2,1,0:T(8,128)(2,1)}) %all-gather.5.cloned.1.call-update) | async-done | bytes 6291472 | tf_op jit(solution)/shard_map/all_gather | solution.py:49
  173.8 3.8 %fusion = bf16[1,48,21,2,128]{4,2,3,1,0:T(8,128)(2,1)S(1)} fusion(bf16[48,2,256,128]{3,2,1,0:T(8,128)(2,1)} %bitcast.51, bf16[48,21,2,256]{3,2,1,0:T(2,128)(2,1)S(1)} %reshape.153), kind=kOutput, calls=%fused_computation.5 | convolution fusion | flops 132378624 | bytes 7839744 | tf_op jit(solution)/shard_map/auncf,ucfb->auncb/dot_general | solution.py:17
  177.6 0.4 copy.26
  178.1 2.0 %gather_fusion.1 = bf16[512,256]{1,0:T(8,128)(2,1)S(1)} fusion(bf16[1008,256]{1,0:T(8,128)(2,1)S(1)} %bitcast.49, s32[1024]{0:T(1024)S(1)} %pad_clamp_fusion), kind=kCustom, calls=%fused_computation.1 | custom fusion | bytes 526336 | tf_op jit(solution)/shard_map/jit(_take)/gather | solution.py:52
  180.1 7.6 %fusion.1 = bf16[512,256]{1,0:T(8,128)(2,1)} fusion(bf16[512,8192]{1,0:T(8,128)(2,1)} %all-gather.3.cloned.1.call-done, bf16[8192,256]{1,0:T(8,128)(2,1)} %param.6, bf16[512,256]{1,0:T(8,128)(2,1)S(1)} %gather_fusion.1, pred[512]{0:T(512)(128)(4,1)S(1)} %get-tuple-element.9), kind=kOutput, calls=%fused_computation.7 | convolution fusion | flops 2148007936 | bytes 13107712 | tf_op jit(solution)/shard_map/dot_general | solution.py:36
  (11 shorter events, 0.2 us)
Async XLA Ops:
  6.5 114.6 %all-gather.3.cloned.1.call-start = ((), (), s32[]{:S(2)}) async-start(), calls=%async_computation | async-start | bytes 8650752 | tf_op jit(solution)/shard_map/all_gather | solution.py:35
  7.3 166.5 %all-gather.5.cloned.1.call-start = ((), (), s32[]{:S(2)}) async-start(), calls=%async_computation.1 | async-start | bytes 6684672 | tf_op jit(solution)/shard_map/all_gather | solution.py:49
Sparse Core Ops, SparseCore 0:
  10.4 110.7 all-gather.2
  123.3 50.4 all-gather.4
where the time goes:
time: 195 us
  waiting for transfers between devices  122 us (63%)
  local copies, waits for them, and re-layouts  42.9 us (22%)
  between operations  13.5 us (7%)
  matrix products  11.4 us (6%)
  other arithmetic  5.09 us (3%)
    all_gather x1, waiting for transfers between devices, local(): features_all = lax.all_gather(tokens, 'tp', axis=1, tiled=True)  106 us
    gather x3, local copies, waits for them, and re-layouts, local(): jnp.take_along_axis(blocks_view, tile_indices[:, :, None], axis=1)  24.6 us
    all_gather x1, waiting for transfers between devices, local(): all_deltas = lax.all_gather(delta, 'rep', axis=0, tiled=True)  14.4 us
    unnamed x3, local copies, waits for them, and re-layouts  10.2 us
    dot_general x1, matrix products, local(): jnp.dot(features_all, base_weight, preferred_element_type=jnp.float32)  7.61 us
  transfers between devices with their start and end apart: 2, of which 2 were waited for; matrix products, arithmetic and copies ran while one was open for 23% of the time, Pallas kernels for 0%

commit v1 on v0

--- a/solution.py
+++ b/solution.py
@@ -2,6 +2,11 @@
 import jax.numpy as jnp
 from jax import lax
 from jax.sharding import PartitionSpec as P
+
+review_the_samples = lambda piece_in: jnp.concatenate(
+    lax.all_to_all(jnp.stack([piece_in for _ in range(lax.axis_size("rep"))], axis=0), "rep", 0, 0),
+    0,
+)
 
 
 def multiply(received, weight_tables):
@@ -46,7 +51,7 @@
         row_count, feat_width
     )
     outgoing = jnp.zeros((variants * capacity, feat_width), jnp.bfloat16).at[slot_index].set(picked)
-    all_deltas = lax.all_gather(delta, "rep", axis=0, tiled=True)
+    all_deltas = review_the_samples(delta)
     returned = multiply(outgoing.reshape(1, variants, capacity, feat_width), all_deltas)
     returned_flat = returned.reshape(variants * capacity, col_blocks * block_size)
     correction_summand = jnp.take(returned_flat, slot_index, axis=0)

time: 195 us -> 184 us (0.944)
  waiting for transfers between devices: 122 us -> 96.2 us
  starting transfers between devices: 0.04 us -> 11.3 us
  local copies, waits for them, and re-layouts: 42.9 us -> 47.6 us
  other arithmetic: 5.09 us -> 3.05 us
    all_gather x1 -> x0, waiting for transfers between devices: 14.4 us -> none  [local(): all_deltas = lax.all_gather(delta, 'rep', axis=0, tiled=True)]
    all_gather x1, waiting for transfers between devices: 106 us -> 92.8 us  [local(): features_all = lax.all_gather(tokens, 'tp', axis=1, tiled=True)]
    all_to_all x0 -> x1, starting transfers between devices: none -> 11.3 us  [lax.all_to_all(jnp.stack([piece_in for _ in range(lax.axis_size('rep'))],...]
    another operation x2 -> x3, local copies, waits for them, and re-layouts: 0.24 us -> 5.49 us  [the longest x1 5.24 us: jnp.stack([piece_in for _ in range(lax.axis_size('rep'))], axis=0)]
    all_to_all x0 -> x1, waiting for transfers between devices: none -> 2.7 us  [lax.all_to_all(jnp.stack([piece_in for _ in range(lax.axis_size('rep'))],...]
    unnamed x3 -> x7, local copies, waits for them, and re-layouts: 10.2 us -> 9.5 us
  transfers between devices with their start and end apart: 2 -> 2, of which waited for: 2 -> 2; matrix products, arithmetic and copies ran while one was open for 23% -> 26% of each run, Pallas kernels for 0% -> 0%
where the time goes in v1:
time: 184 us; the launch traced here: 183 us
  waiting for transfers between devices  96.2 us (52%)
  local copies, waits for them, and re-layouts  47.6 us (26%)
  between operations  13.5 us (7%)
  matrix products  11.4 us (6%)
  starting transfers between devices  11.3 us (6%)
  other arithmetic  3.05 us (2%)
    all_gather x1, waiting for transfers between devices, local(): features_all = lax.all_gather(tokens, 'tp', axis=1, tiled=True)  92.8 us
    gather x3, local copies, waits for them, and re-layouts, local(): jnp.take_along_axis(blocks_view, tile_indices[:, :, None], axis=1)  24.6 us
    all_to_all x1, starting transfers between devices, lax.all_to_all(jnp.stack([piece_in for _ in range(lax.axis_size('rep'))],...  11.3 us
    unnamed x7, local copies, waits for them, and re-layouts  9.5 us
    dot_general x1, matrix products, local(): jnp.dot(features_all, base_weight, preferred_element_type=jnp.float32)  7.61 us
    another operation x1, local copies, waits for them, and re-layouts, jnp.stack([piece_in for _ in range(lax.axis_size('rep'))], axis=0)  5.24 us
    dot_general x1, matrix products, multiply(): jnp.einsum('auncf,ucfb->auncb', shaped, flat_weights, preferred_element_t...  3.82 us
  transfers between devices with their start and end apart: 2, of which 2 were waited for; matrix products, arithmetic and copies ran while one was open for 26% of the time, Pallas kernels for 0%

profile of v1, /device:TPU:1, one launch (start us, length us, event | category | flops | bytes accessed | tf_op | source)
XLA Modules:
  0.0 183.1 jit_solution(10730475682341761476)
XLA Ops:
  6.5 0.7 all-gather.2.cloned.1.call-update
  7.3 5.2 %stack.2 = bf16[16,3,2,2,128,128]{5,4,3,2,1,0:T(8,128)(2,1)} broadcast(bf16[3,2,2,128,128]{4,3,2,1,0:T(8,128)(2,1)} %param.7), dimensions={1,2,3,4,5} | broadcast | bytes 6684672 | tf_op jit(solution)/shard_map/stack | solution.py:7
  12.5 11.3 %all-to-all-start = ((bf16[16,3,2,2,128,128]{5,4,3,2,1,0:T(8,128)(2,1)}), bf16[16,3,2,2,128,128]{5,4,3,2,1,0:T(8,128)(2,1)}, u32[]{:S(2)}, u32[]{:S(2)}) async-start(bf16[16,3,2,2,128,128]{5,4,3,2,1,0:T(8,128)(2,1)} %stack.2), calls=%async_computation | async-start | bytes 12582912 | tf_op jit(solution)/shard_map/all_to_all | solution.py:7
  23.9 1.2 reduce-window.6
  25.1 0.2 slice_reduce_fusion
  25.3 0.1 copy.12
  25.4 0.1 fusion.8
  25.6 2.1 %gather_fusion = s32[512,2,2]{2,1,0:T(2,128)S(1)} fusion(s32[48,2,2]{2,1,0:T(2,128)S(1)} %copy.12, s32[1024]{0:T(1024)S(1)} %pad_clamp_fusion.1), kind=kCustom, calls=%fused_computation | custom fusion | bytes 18432 | tf_op jit(solution)/shard_map/jit(_take)/gather | solution.py:46
  27.7 0.2 copy.13
  27.9 0.1 copy.16
  28.1 0.2 reshape.169
  28.3 0.2 copy.14
  28.5 92.8 %all-gather.2.cloned.1.call-done = bf16[512,8192]{1,0:T(8,128)(2,1)} async-done(((bf16[512,256]{1,0:T(8,128)(2,1)}), bf16[512,8192]{1,0:T(8,128)(2,1)}) %all-gather.2.cloned.1.call-update) | async-done | bytes 8388624 | tf_op jit(solution)/shard_map/all_gather | solution.py:40
  121.3 9.3 %copy.20 = bf16[64,8,64,128]{3,2,1,0:T(8,128)(2,1)} copy(bf16[64,8,64,128]{3,1,2,0:T(8,128)(2,1)} %bitcast.50) | data formatting | bytes 16777216
  130.6 24.3 %gather_fusion.2 = bf16[2048,128]{1,0:T(8,128)(2,1)S(1)} fusion(bf16[512,64,128]{2,1,0:T(8,128)(2,1)} %bitcast.48, s32[2048]{0:T(1024)S(1)} %reshape.169), kind=kCustom, calls=%fused_computation.2 | custom fusion | bytes 1064960 | tf_op jit(solution)/shard_map/jit(take_along_axis)/gather | solution.py:50
  154.9 1.6 broadcast_select_fusion
  156.6 2.9 %scatter_custom_fusion = bf16[1008,512]{1,0:T(8,128)(2,1)S(1)} fusion(s32[512]{0:T(512)S(1)} %bitcast.57, bf16[64,8,4,128]{3,2,1,0:T(4,128)(2,1)S(1)} %bitcast.51, bf16[]{:T(256)} %constant.50.clone.1), kind=kCustom, calls=%fused_computation.9 | custom fusion | bytes 1556482 | tf_op jit(solution)/shard_map/scatter | solution.py:53
  159.4 0.2 reshape.152
  159.7 2.7 %all-to-all-done = bf16[16,3,2,2,128,128]{5,4,3,2,1,0:T(8,128)(2,1)} async-done(((bf16[16,3,2,2,128,128]{5,4,3,2,1,0:T(8,128)(2,1)}), bf16[16,3,2,2,128,128]{5,4,3,2,1,0:T(8,128)(2,1)}, u32[]{:S(2)}, u32[]{:S(2)}) %all-to-all-start) | async-done | bytes 6291488 | tf_op jit(solution)/shard_map/all_to_all | solution.py:7
  162.4 3.8 %fusion = bf16[1,48,21,2,128]{4,2,3,1,0:T(8,128)(2,1)S(1)} fusion(bf16[48,2,256,128]{3,2,1,0:T(8,128)(2,1)} %bitcast.7, bf16[48,21,2,256]{3,2,1,0:T(2,128)(2,1)S(1)} %reshape.152), kind=kOutput, calls=%fused_computation.5 | convolution fusion | flops 132378624 | bytes 7839744 | tf_op jit(solution)/shard_map/auncf,ucfb->auncb/dot_general | solution.py:22
  166.2 0.4 copy.18
  166.6 0.1 copy.31
  166.7 2.0 %gather_fusion.1 = bf16[512,256]{1,0:T(8,128)(2,1)S(1)} fusion(bf16[1008,256]{1,0:T(8,128)(2,1)S(1)} %bitcast.49, s32[1024]{0:T(1024)S(1)} %pad_clamp_fusion), kind=kCustom, calls=%fused_computation.1 | custom fusion | bytes 526336 | tf_op jit(solution)/shard_map/jit(_take)/gather | solution.py:57
  168.7 7.6 %fusion.1 = bf16[512,256]{1,0:T(8,128)(2,1)} fusion(bf16[512,8192]{1,0:T(8,128)(2,1)} %all-gather.2.cloned.1.call-done, bf16[8192,256]{1,0:T(8,128)(2,1)} %param.6, bf16[512,256]{1,0:T(8,128)(2,1)S(1)} %gather_fusion.1, pred[512]{0:T(512)(128)(4,1)S(1)} %get-tuple-element.9), kind=kOutput, calls=%fused_computation.7 | convolution fusion | flops 2148007936 | bytes 13107712 | tf_op jit(solution)/shard_map/dot_general | solution.py:41
  (15 shorter events, 0.2 us)
Async XLA Ops:
  6.5 114.8 %all-gather.2.cloned.1.call-start = ((), (), s32[]{:S(2)}) async-start(), calls=%async_computation.1 | async-start | bytes 8650752 | tf_op jit(solution)/shard_map/all_gather | solution.py:40
  12.5 11.3 %copy-start = (s32[512,1]{0,1:T(1,128)S(1)}, s32[512,1]{0,1:T(1,128)}, u32[]{:S(2)}) copy-start(s32[512,1]{0,1:T(1,128)} %param.9) | copy-start | bytes 6148
  12.5 12.8 %copy-start.1 = (s32[48,2,2]{0,2,1:T(2,128)S(1)}, s32[48,2,2]{0,2,1:T(2,128)}, u32[]{:S(2)}) copy-start(s32[48,2,2]{0,2,1:T(2,128)} %param.8) | copy-start | bytes 2308
  12.5 149.9 %all-to-all-start = ((bf16[16,3,2,2,128,128]{5,4,3,2,1,0:T(8,128)(2,1)}), bf16[16,3,2,2,128,128]{5,4,3,2,1,0:T(8,128)(2,1)}, u32[]{:S(2)}, u32[]{:S(2)}) async-start(bf16[16,3,2,2,128,128]{5,4,3,2,1,0:T(8,128)(2,1)} %stack.2), calls=%async_computation | async-start | bytes 12582912 | tf_op jit(solution)/shard_map/all_to_all | solution.py:7
Sparse Core Ops, SparseCore 0:
  10.4 110.8 all-gather.1
